TPU v7x, 32 devices: a whole 2x2x4 slice. The times are simulated.
32 devices in a mesh: groups: 2 (over y), wide: 4 (over z), narrow: 4 (over x, core).
Axes of the slice: x: 2, y: 2, z: 4, core: 2. Of those that a mesh axis runs over, the one named last changes fastest.
Arguments:
- hidden: bfloat16 [32, 8192], P('groups', 'wide'), parts along dimension 0, may hold values from -6 to 6
- w_query: bfloat16 [8192, 8192], P('wide', 'narrow'), may hold values from -0.0625 to 0.0625
- w_key: bfloat16 [8192, 1024], P('wide', 'narrow'), may hold values from -0.0625 to 0.0625
- w_value: bfloat16 [8192, 1024], P('wide', 'narrow'), may hold values from -0.0625 to 0.0625
- w_out: bfloat16 [8192, 8192], P('narrow', 'wide'), may hold values from -0.0625 to 0.0625
- key_cache: bfloat16 [32, 768, 8, 128], P(('groups', 'wide'), None, 'narrow'), parts along dimension 0, may hold values from -720 to 720
- value_cache: bfloat16 [32, 768, 8, 128], P(('groups', 'wide'), None, 'narrow'), parts along dimension 0, may hold values from -6 to 6
- cycle_offset: int32 [32], P(('groups', 'wide')), parts along dimension 0, may hold values from 0 to 767
- valid_length: int32 [32], P(('groups', 'wide')), parts along dimension 0, may hold values from 1 to 768, as said below
- slot_of: int32 [32], P('groups'), parts along dimension 0, may hold values from 0 to 15, as said below
Outputs:
- attn_out: bfloat16 [32, 8192], P('groups', 'wide'), parts along dimension 0
- new_keys: bfloat16 [32, 1024], P(('groups', 'wide'), 'narrow'), parts along dimension 0
- new_values: bfloat16 [32, 1024], P(('groups', 'wide'), 'narrow'), parts along dimension 0
There are 2 independent parts, one for each index of `groups`. A program takes and returns all parts, laid end to end along the dimension named above; an argument that names none is the same for every part. Nothing has to cross between parts.
Inputs may be any that keep to these rules, and one draw needn't show every extreme that they name: Requests are in 4 microbatches of consecutive rows; each cache owner (a block of 4 consecutive slots) holds exactly 1 request of each microbatch m, at the slots owner * 4 + m + j for 0 <= j < 1; slot_of is a permutation. `valid_length`: at least one slot has a full cycle.
All inputs are finite; a program needn't handle non-finite values.
Results may differ from a plain program's by a relative error of at most 0.012.
Values may be sent and summed in bfloat16 or wider, within the bound.
A program may use at most 64 MiB of HBM per device.

v0:
```python
import jax
import jax.numpy as jnp
from jax import lax
from jax.sharding import PartitionSpec as P

masked_low = -1e30


def attend(queries, keys_new, values_new, key_cache, value_cache, offset, length):
    slots, window, kv_local, head_dim = key_cache.shape
    group = queries.shape[1] // (kv_local * head_dim)
    scale = 1.0 / jnp.sqrt(jnp.float32(head_dim))
    query_heads = queries.reshape(slots, kv_local, group, head_dim)
    key_heads = keys_new.reshape(slots, kv_local, head_dim)
    value_heads = values_new.reshape(slots, kv_local, head_dim)
    cached = (
        jnp.einsum("skgd,sjkd->skgj", query_heads, key_cache, preferred_element_type=jnp.float32)
        * scale
    )
    fresh = (
        jnp.einsum("skgd,skd->skg", query_heads, key_heads, preferred_element_type=jnp.float32)
        * scale
    )
    distance = (offset[:, None] - jnp.arange(window, dtype=jnp.int32)[None, :]) % window
    usable = ((distance > 0) & (distance < length[:, None]))[:, None, None, :]
    masked = jnp.where(usable, cached, masked_low)
    top = jnp.maximum(jnp.max(masked, axis=3), fresh)
    spread = jnp.where(usable, jnp.exp(masked - top[..., None]), 0.0)
    own = jnp.exp(fresh - top)
    total = jnp.sum(spread, axis=3) + own
    weights = (spread / total[..., None]).astype(jnp.bfloat16)
    own_weight = (own / total).astype(jnp.bfloat16)
    mixed = jnp.einsum("skgj,sjkd->skgd", weights, value_cache, preferred_element_type=jnp.float32)
    mixed = (
        mixed
        + own_weight.astype(jnp.float32)[..., None] * value_heads.astype(jnp.float32)[:, :, None, :]
    )
    return mixed.astype(jnp.bfloat16).reshape(slots, -1)


def per_device(
    hidden,
    w_query,
    w_key,
    w_value,
    w_out,
    key_cache,
    value_cache,
    cycle_offset,
    valid_length,
    slot_of,
):
    requests = slot_of.shape[0]
    slots_dev = key_cache.shape[0]
    query_cols = w_query.shape[1]
    key_cols = w_key.shape[1]
    order = jnp.zeros((requests,), jnp.int32).at[slot_of].set(jnp.arange(requests, dtype=jnp.int32))
    rows = hidden[order[jnp.arange(slots_dev * lax.axis_size("wide"), dtype=jnp.int32)]]
    summed = lax.psum_scatter(
        jnp.concatenate(
            [
                jnp.dot(rows, w_query, preferred_element_type=jnp.float32),
                jnp.dot(rows, w_key, preferred_element_type=jnp.float32),
                jnp.dot(rows, w_value, preferred_element_type=jnp.float32),
            ],
            axis=1,
        ),
        "wide",
        scatter_dimension=0,
        tiled=True,
    )
    fresh = summed.astype(jnp.bfloat16)
    queries = fresh[:, :query_cols]
    keys_out = fresh[:, query_cols : query_cols + key_cols]
    values_out = fresh[:, query_cols + key_cols :]
    heads = attend(
        queries, keys_out, values_out, key_cache, value_cache, cycle_offset, valid_length
    )
    slot_out = jnp.dot(
        lax.all_gather(heads, "wide", axis=0, tiled=True), w_out, preferred_element_type=jnp.float32
    )
    request_out = slot_out[slot_of]
    attn_out = lax.psum(request_out, "narrow").astype(jnp.bfloat16)
    return (attn_out, keys_out, values_out)


def solution(mesh):
    placed = (
        P("groups", "wide"),
        P("wide", "narrow"),
        P("wide", "narrow"),
        P("wide", "narrow"),
        P("narrow", "wide"),
        P(("groups", "wide"), None, "narrow", None),
        P(("groups", "wide"), None, "narrow", None),
        P(("groups", "wide")),
        P(("groups", "wide")),
        P("groups"),
    )
    return jax.shard_map(
        per_device,
        mesh=mesh,
        in_specs=placed,
        out_specs=(
            P("groups", "wide"),
            P(("groups", "wide"), "narrow"),
            P(("groups", "wide"), "narrow"),
        ),
        check_vma=False,
    )
```

profile of v0, /device:TPU:0, one launch (start us, length us, event | category | flops | bytes accessed | tf_op | source)
XLA Modules:
  0.0 66.5 jit_solution(1026639459956276129)
XLA Ops:
  0.6 0.0 copy-start
  0.6 0.8 %compare_select_fusion.1 = s32[16]{0:T(128)S(1)} fusion(s32[16]{0:T(128)} %param.19), kind=kLoop, calls=%fused_computation.40 | loop fusion | flops 48 | bytes 128 | tf_op jit(solution)/shard_map/select_n | solution.py:57
  1.4 0.6 scatter_custom_fusion
  2.1 0.7 gather_fusion
  2.8 1.5 %gather_fusion.1 = bf16[16,2048]{1,0:T(8,128)(2,1)S(1)} fusion(bf16[16,2048]{1,0:T(8,128)(2,1)} %param.10, s32[1024]{0:T(1024)S(1)} %pad_clamp_fusion.1), kind=kCustom, calls=%fused_computation.1 | custom fusion | bytes 131136 | tf_op jit(solution)/shard_map/gather | solution.py:58
  4.3 0.0 copy-start.1
  4.3 0.0 copy-start.2
  4.3 4.7 %fusion.37 = f32[16,2048]{1,0:T(8,128)S(1)} fusion(bf16[16,2048]{1,0:T(8,128)(2,1)S(1)} %gather_fusion.1, bf16[2048,2048]{1,0:T(8,128)(2,1)} %param.11), kind=kOutput, calls=%fused_computation.49 | convolution fusion | flops 134217728 | bytes 8585216 | tf_op jit(solution)/shard_map/dot_general | solution.py:62
  9.0 0.0 copy-done.1
  9.0 0.0 copy-start.8
  9.0 0.0 copy-start.5
  9.0 0.0 copy-start.6
  9.0 0.2 fusion.38
  9.3 0.0 copy-done.2
  9.3 0.3 fusion.39
  9.6 0.0 copy-start.7
  9.6 23.6 %all-reduce.3 = bf16[16,2560]{1,0:T(8,128)(2,1)S(1)} all-reduce(f32[16,2560]{1,0:T(8,128)S(1)} %pad_maximum_fusion), channel_id=2, replica_groups=mesh['groups'=2,'wide'=4,'narrow'=4] {'wide'}, use_global_device_ids=true, to_apply=%region_1.0.clone | all-reduce | flops 40960 | bytes 245760
  33.2 0.0 copy-done.8
  33.2 0.6 dynamic-slice
  34.5 0.0 copy-start.3
  34.5 0.0 copy-start.4
  34.5 0.1 fusion.21
  34.7 0.0 copy-done.5
  34.7 0.0 copy-done.6
  34.7 0.1 compare_and_fusion
  34.8 0.0 copy-done
  34.8 0.6 fusion.36
  35.4 0.2 fusion.16
  35.6 0.0 copy-done.7
  35.6 0.4 fusion.13
  36.0 0.0 copy-done.3
  36.0 0.0 copy-done.4
  36.1 13.2 %all-gather = bf16[4,4,2048]{2,1,0:T(4,128)(2,1)S(1)} all-gather(bf16[1,4,2048]{2,1,0:T(4,128)(2,1)S(1)} %reshape.114), channel_id=1, replica_groups=mesh['groups'=2,'wide'=4,'narrow'=4] {'wide'}, dimensions={0}, use_global_device_ids=true | all-gather | bytes 81920 | tf_op jit(solution)/shard_map/all_gather | solution.py:80
  49.3 4.6 %fusion.40 = f32[16,2048]{1,0:T(8,128)S(1)} fusion(bf16[16,2048]{1,0:T(8,128)(2,1)S(1)} %reshape.115, bf16[2048,2048]{1,0:T(8,128)(2,1)} %param.14), kind=kOutput, calls=%fused_computation.52 | convolution fusion | flops 134217728 | bytes 8585216 | tf_op jit(solution)/shard_map/dot_general | solution.py:79
  53.9 0.6 gather_fusion.2
  54.5 12.0 %all-reduce.4 = bf16[16,2048]{1,0:T(8,128)(2,1)} all-reduce(f32[16,2048]{1,0:T(8,128)S(1)} %gather_fusion.2), channel_id=1, replica_groups=mesh['groups'=2,'wide'=4,'narrow'=4] {'narrow'}, use_global_device_ids=true, to_apply=%region_4.5 | all-reduce | flops 32768 | bytes 196608 | tf_op jit(solution)/shard_map/psum | solution.py:83
  (16 shorter events, 0.2 us)
Async XLA Ops:
  0.6 34.1 %copy-start = (bf16[4,768,2,128]{3,2,1,0:T(2,128)(2,1)S(1)}, bf16[4,768,2,128]{3,2,1,0:T(2,128)(2,1)}, u32[]{:S(2)}) copy-start(bf16[4,768,2,128]{3,2,1,0:T(2,128)(2,1)} %param.15) | copy-start | bytes 4718596
  4.3 4.7 %copy-start.1 = (bf16[2048,256]{1,0:T(8,128)(2,1)S(1)}, bf16[2048,256]{1,0:T(8,128)(2,1)}, u32[]{:S(2)}) copy-start(bf16[2048,256]{1,0:T(8,128)(2,1)} %param.12) | copy-start | bytes 3145732
  4.3 5.0 %copy-start.2 = (bf16[2048,256]{1,0:T(8,128)(2,1)S(1)}, bf16[2048,256]{1,0:T(8,128)(2,1)}, u32[]{:S(2)}) copy-start(bf16[2048,256]{1,0:T(8,128)(2,1)} %param.13) | copy-start | bytes 3145732
  9.0 24.2 %copy-start.8 = (u32[32]{0:T(128)S(1)}, u32[32]{0:T(128)}, u32[]{:S(2)}) copy-start(u32[32]{0:T(128)} %constant.32) | copy-start | bytes 388
  9.0 25.6 %copy-start.5 = (s32[4]{0:T(128)S(1)}, s32[4]{0:T(128)}, u32[]{:S(2)}) copy-start(s32[4]{0:T(128)} %param.18) | copy-start | bytes 52
  9.0 25.6 %copy-start.6 = (s32[4]{0:T(128)S(1)}, s32[4]{0:T(128)}, u32[]{:S(2)}) copy-start(s32[4]{0:T(128)} %param.17) | copy-start | bytes 52
  9.6 26.1 %copy-start.7 = (bf16[4,768,2,128]{3,2,1,0:T(2,128)(2,1)S(1)}, bf16[4,768,2,128]{3,2,1,0:T(2,128)(2,1)}, u32[]{:S(2)}) copy-start(bf16[4,768,2,128]{3,2,1,0:T(2,128)(2,1)} %param.16) | copy-start | bytes 4718596
  34.5 1.6 %copy-start.3 = (bf16[4,256]{1,0:T(4,128)(2,1)}, bf16[4,256]{1,0:T(4,128)(2,1)S(1)}, u32[]{:S(2)}) copy-start(bf16[4,256]{1,0:T(4,128)(2,1)S(1)} %get-tuple-element.3) | copy-start | bytes 6148
  34.5 1.5 %copy-start.4 = (bf16[4,256]{1,0:T(4,128)(2,1)}, bf16[4,256]{1,0:T(4,128)(2,1)S(1)}, u32[]{:S(2)}) copy-start(bf16[4,256]{1,0:T(4,128)(2,1)S(1)} %get-tuple-element.4) | copy-start | bytes 6148
where the time goes:
time: 66.8 us; the launch traced here: 66.5 us
  blocking collectives  48.9 us (73%)
  matrix products  10.9 us (16%)
  local copies, waits for them, and re-layouts  4.13 us (6%)
  between operations  1.5 us (2%)
  other arithmetic  1.13 us (2%)
    unnamed x1, blocking collectives  23.6 us
    all_gather x1, blocking collectives, per_device(): lax.all_gather(heads, 'wide', axis=0, tiled=True)  13.2 us
    psum x1, blocking collectives, per_device(): attn_out = lax.psum(request_out, 'narrow').astype(jnp.bfloat16)  12 us
    dot_general x1, matrix products, per_device(): jnp.dot(rows, w_query, preferred_element_type=jnp.float32)  4.72 us
    dot_general x1, matrix products, per_device(): jnp.dot(lax.all_gather(heads, 'wide', axis=0, tiled=True), w_out, preferr...  4.58 us
    gather x1, local copies, waits for them, and re-layouts, per_device(): hidden[order[jnp.arange(slots_dev * lax.axis_size('wide'), dtype=jnp.int3...  1.51 us

commit v1 on v0

v1 whole, which is shorter than its diff:
```python
import functools

import jax
import jax.numpy as jnp
from jax import lax
from jax.experimental import pallas as pl
from jax.experimental.pallas import tpu as pltpu
from jax.sharding import PartitionSpec as P

masked_low = -1e30
MESH = pl.DeviceIdType.MESH


def width_of(columns, most):
    width = min(columns, most)
    while columns % width:
        width -= 128
    return width


def kernel(
    wide,
    narrow,
    kv_local,
    q_width,
    o_width,
    hidden,
    w_query,
    w_key,
    w_value,
    w_out,
    key_cache,
    value_cache,
    slot_row,
    cycle_offset,
    valid_length,
    attn_out,
    new_keys,
    new_values,
    wq,
    wk,
    wv,
    wo,
    keys,
    values,
    part,
    got,
    query_heads,
    mixed_heads,
    heads_own,
    heads_got,
    heads_full,
    out_part,
    out_got,
    in_sem,
    send_sem,
    recv_sem,
    head_send,
    head_recv,
    out_send,
    out_recv,
):
    me_wide = lax.axis_index("wide")
    me_narrow = lax.axis_index("narrow")
    requests = hidden.shape[0]
    slots = keys.shape[0]
    head_dim = keys.shape[2]
    span = keys.shape[1]
    window = span // kv_local
    query_cols = wq.shape[1]
    key_cols = wk.shape[1]
    out_cols = wo.shape[1]
    heads_local = query_cols // head_dim
    group = heads_local // kv_local
    q_chunks = query_cols // q_width
    o_chunks = out_cols // o_width

    first = [
        pltpu.make_async_copy(w_key, wk, in_sem.at[0]),
        pltpu.make_async_copy(w_value, wv, in_sem.at[1]),
    ]
    for c in range(q_chunks):
        cols = pl.ds(c * q_width, q_width)
        first.append(pltpu.make_async_copy(w_query.at[:, cols], wq.at[:, cols], in_sem.at[2 + c]))
    base = 2 + q_chunks
    cache_in = [
        pltpu.make_async_copy(key_cache, keys, in_sem.at[base]),
        pltpu.make_async_copy(value_cache, values, in_sem.at[base + 1]),
    ]
    out_in = []
    for c in range(o_chunks):
        cols = pl.ds(c * o_width, o_width)
        out_in.append(
            pltpu.make_async_copy(w_out.at[:, cols], wo.at[:, cols], in_sem.at[base + 2 + c])
        )
    for copy in first:
        copy.start()

    barrier = pltpu.get_barrier_semaphore()
    for d in range(1, wide):
        pl.semaphore_signal(
            barrier,
            inc=1,
            device_id={"wide": lax.rem(me_wide + d, wide)},
            device_id_type=MESH,
        )
    for d in range(1, narrow):
        pl.semaphore_signal(
            barrier,
            inc=1,
            device_id={"narrow": lax.rem(me_narrow + d, narrow)},
            device_id_type=MESH,
        )

    slot_id = lax.broadcasted_iota(jnp.int32, (requests, requests), 0)
    pick = jnp.where(slot_row[...] == slot_id, 1.0, 0.0)
    rows = jnp.dot(
        pick.astype(jnp.bfloat16), hidden[...], preferred_element_type=jnp.float32
    ).astype(jnp.bfloat16)

    def to_owner(block, d, col, width):
        peer = lax.rem(me_wide + d, wide)
        return pltpu.make_async_remote_copy(
            src_ref=part.at[peer, :, pl.ds(col, width)],
            dst_ref=got.at[d, :, pl.ds(col, width)],
            send_sem=send_sem.at[block, d],
            recv_sem=recv_sem.at[block, d],
            device_id={"wide": peer},
            device_id_type=MESH,
        )

    blocks = [(query_cols, 2 * key_cols)] + [(c * q_width, q_width) for c in range(q_chunks)]
    for block, (col, width) in enumerate(blocks):
        if block == 0:
            first[0].wait()
            sums = jnp.dot(rows, wk[...], preferred_element_type=jnp.float32)
            for w in range(wide):
                part[w, :, col : col + key_cols] = sums[w * slots : (w + 1) * slots]
            first[1].wait()
            sums = jnp.dot(rows, wv[...], preferred_element_type=jnp.float32)
            for w in range(wide):
                part[w, :, col + key_cols : col + width] = sums[w * slots : (w + 1) * slots]
            pl.semaphore_wait(barrier, wide + narrow - 2)
        else:
            first[1 + block].wait()
            sums = jnp.dot(rows, wq[:, col : col + width], preferred_element_type=jnp.float32)
            for w in range(wide):
                part[w, :, col : col + width] = sums[w * slots : (w + 1) * slots]
        for d in range(1, wide):
            to_owner(block, d, col, width).start()
    for copy in cache_in + out_in:
        copy.start()

    place = lax.broadcasted_iota(jnp.int32, (1, span), 1)
    position = place // kv_local
    kv_of = place - position * kv_local
    row_kv = lax.broadcasted_iota(jnp.int32, (heads_local, 1), 0) // group
    same_head = row_kv == kv_of
    scale = 1.0 / jnp.sqrt(jnp.float32(head_dim))

    def summed(col, width):
        total = part[me_wide, :, col : col + width]
        for d in range(1, wide):
            total = total + got[d, :, col : col + width]
        return total

    for d in range(1, wide):
        to_owner(0, d, *blocks[0]).wait_recv()
    keys_new = summed(query_cols, key_cols).astype(jnp.bfloat16)
    values_new = summed(query_cols + key_cols, key_cols).astype(jnp.bfloat16)
    new_keys[...] = keys_new
    new_values[...] = values_new
    keys_fresh = keys_new.astype(jnp.float32)
    values_fresh = values_new.astype(jnp.float32)
    for block in range(1, len(blocks)):
        col, width = blocks[block]
        for d in range(1, wide):
            to_owner(block, d, col, width).wait_recv()
        for h in range(col // head_dim, (col + width) // head_dim):
            query_heads[:, h, :] = summed(h * head_dim, head_dim)

    for copy in cache_in:
        copy.wait()

    def by_head(fresh, s):
        result = jnp.broadcast_to(fresh[s : s + 1, :head_dim], (heads_local, head_dim))
        for k in range(1, kv_local):
            other = fresh[s : s + 1, k * head_dim : (k + 1) * head_dim]
            result = jnp.where(row_kv == k, other, result)
        return result

    for s in range(slots):
        query = query_heads[s].astype(jnp.bfloat16)
        scores = (
            lax.dot_general(
                query, keys[s], (((1,), (1,)), ((), ())), preferred_element_type=jnp.float32
            )
            * scale
        )
        own_score = (
            jnp.sum(query.astype(jnp.float32) * by_head(keys_fresh, s), axis=1, keepdims=True)
            * scale
        )
        offset = cycle_offset[s]
        distance = offset - position
        distance = jnp.where(distance < 0, distance + window, distance)
        usable = (distance > 0) & (distance < valid_length[s])
        masked = jnp.where(usable & same_head, scores, masked_low)
        top = jnp.maximum(jnp.max(masked, axis=1, keepdims=True), own_score)
        spread = jnp.exp(masked - top)
        own = jnp.exp(own_score - top)
        inverse = 1.0 / (jnp.sum(spread, axis=1, keepdims=True) + own)
        mixed = jnp.dot(
            (spread * inverse).astype(jnp.bfloat16), values[s], preferred_element_type=jnp.float32
        )
        own_weight = (own * inverse).astype(jnp.bfloat16).astype(jnp.float32)
        mixed_heads[s] = mixed + own_weight * by_head(values_fresh, s)

    for h in range(heads_local):
        heads_own[:, h * head_dim : (h + 1) * head_dim] = mixed_heads[:, h, :].astype(jnp.bfloat16)

    def to_wide(d):
        return pltpu.make_async_remote_copy(
            src_ref=heads_own,
            dst_ref=heads_got.at[d],
            send_sem=head_send.at[d],
            recv_sem=head_recv.at[d],
            device_id={"wide": lax.rem(me_wide + d, wide)},
            device_id_type=MESH,
        )

    for d in range(1, wide):
        to_wide(d).start()
    heads_full[0:slots] = heads_own[...].astype(jnp.float32)
    for d in range(1, wide):
        to_wide(d).wait_recv()
        heads_full[d * slots : (d + 1) * slots] = heads_got[d].astype(jnp.float32)
    held_row = lax.broadcasted_iota(jnp.int32, (requests, requests), 0)
    back = held_row // slots
    held_slot = lax.rem(me_wide - back + wide, wide) * slots + (held_row - back * slots)
    give = jnp.where(slot_row[...] == held_slot, 1.0, 0.0).astype(jnp.bfloat16)
    heads = lax.dot_general(
        give,
        heads_full[...].astype(jnp.bfloat16),
        (((0,), (0,)), ((), ())),
        preferred_element_type=jnp.float32,
    ).astype(jnp.bfloat16)

    def to_narrow(c, d):
        return pltpu.make_async_remote_copy(
            src_ref=out_part.at[c],
            dst_ref=out_got.at[c, me_narrow],
            send_sem=out_send.at[c, d],
            recv_sem=out_recv.at[c, d],
            device_id={"narrow": lax.rem(me_narrow + d, narrow)},
            device_id_type=MESH,
        )

    for c in range(o_chunks):
        cols = slice(c * o_width, (c + 1) * o_width)
        out_in[c].wait()
        sums = jnp.dot(heads, wo[:, cols], preferred_element_type=jnp.float32)
        out_part[c] = sums.astype(jnp.bfloat16)
        for d in range(1, narrow):
            to_narrow(c, d).start()
        out_got[c, me_narrow] = sums.astype(jnp.bfloat16)
    for c in range(o_chunks):
        cols = slice(c * o_width, (c + 1) * o_width)
        for d in range(1, narrow):
            to_narrow(c, d).wait_recv()
        total = out_got[c, 0].astype(jnp.float32)
        for n in range(1, narrow):
            total = total + out_got[c, n].astype(jnp.float32)
        attn_out[:, cols] = total.astype(jnp.bfloat16)

    for block, (col, width) in enumerate(blocks):
        for d in range(1, wide):
            to_owner(block, d, col, width).wait_send()
    for d in range(1, wide):
        to_wide(d).wait_send()
    for c in range(o_chunks):
        for d in range(1, narrow):
            to_narrow(c, d).wait_send()


def per_device(
    wide,
    narrow,
    hidden,
    w_query,
    w_key,
    w_value,
    w_out,
    key_cache,
    value_cache,
    cycle_offset,
    valid_length,
    slot_of,
):
    requests = slot_of.shape[0]
    slots, window, kv_local, head_dim = key_cache.shape
    query_cols = w_query.shape[1]
    key_cols = w_key.shape[1]
    out_cols = w_out.shape[1]
    q_width = width_of(query_cols, 512)
    o_width = width_of(out_cols, 512)
    q_chunks = query_cols // q_width
    o_chunks = out_cols // o_width
    all_cols = query_cols + 2 * key_cols
    span = window * kv_local
    vmem = pl.BlockSpec(memory_space=pltpu.VMEM)
    smem = pl.BlockSpec(memory_space=pltpu.SMEM)
    anywhere = pl.BlockSpec(memory_space=pl.ANY)
    return pl.pallas_call(
        functools.partial(kernel, wide, narrow, kv_local, q_width, o_width),
        out_shape=(
            jax.ShapeDtypeStruct((requests, out_cols), jnp.bfloat16),
            jax.ShapeDtypeStruct((slots, key_cols), jnp.bfloat16),
            jax.ShapeDtypeStruct((slots, key_cols), jnp.bfloat16),
        ),
        in_specs=[vmem] + [anywhere] * 6 + [vmem, smem, smem],
        out_specs=(vmem, vmem, vmem),
        scratch_shapes=[
            pltpu.VMEM(w_query.shape, jnp.bfloat16),
            pltpu.VMEM(w_key.shape, jnp.bfloat16),
            pltpu.VMEM(w_value.shape, jnp.bfloat16),
            pltpu.VMEM(w_out.shape, jnp.bfloat16),
            pltpu.VMEM((slots, span, head_dim), jnp.bfloat16),
            pltpu.VMEM((slots, span, head_dim), jnp.bfloat16),
            pltpu.VMEM((wide, slots, all_cols), jnp.float32),
            pltpu.VMEM((wide, slots, all_cols), jnp.float32),
            pltpu.VMEM((slots, query_cols // head_dim, head_dim), jnp.float32),
            pltpu.VMEM((slots, query_cols // head_dim, head_dim), jnp.float32),
            pltpu.VMEM((slots, query_cols), jnp.bfloat16),
            pltpu.VMEM((wide, slots, query_cols), jnp.bfloat16),
            pltpu.VMEM((wide * slots, query_cols), jnp.float32),
            pltpu.VMEM((o_chunks, requests, o_width), jnp.bfloat16),
            pltpu.VMEM((o_chunks, narrow, requests, o_width), jnp.bfloat16),
            pltpu.SemaphoreType.DMA((4 + q_chunks + o_chunks,)),
            pltpu.SemaphoreType.DMA((1 + q_chunks, wide)),
            pltpu.SemaphoreType.DMA((1 + q_chunks, wide)),
            pltpu.SemaphoreType.DMA((wide,)),
            pltpu.SemaphoreType.DMA((wide,)),
            pltpu.SemaphoreType.DMA((o_chunks, narrow)),
            pltpu.SemaphoreType.DMA((o_chunks, narrow)),
        ],
        compiler_params=pltpu.CompilerParams(
            collective_id=0, has_side_effects=True, vmem_limit_bytes=60 * 1024 * 1024
        ),
        name="decode_step",
    )(
        hidden,
        w_query,
        w_key,
        w_value,
        w_out,
        key_cache.reshape(slots, span, head_dim),
        value_cache.reshape(slots, span, head_dim),
        slot_of.reshape(1, requests),
        cycle_offset,
        valid_length,
    )


def solution(mesh):
    placed = (
        P("groups", "wide"),
        P("wide", "narrow"),
        P("wide", "narrow"),
        P("wide", "narrow"),
        P("narrow", "wide"),
        P(("groups", "wide"), None, "narrow", None),
        P(("groups", "wide"), None, "narrow", None),
        P(("groups", "wide")),
        P(("groups", "wide")),
        P("groups"),
    )
    return jax.shard_map(
        functools.partial(per_device, mesh.shape["wide"], mesh.shape["narrow"]),
        mesh=mesh,
        in_specs=placed,
        out_specs=(
            P("groups", "wide"),
            P(("groups", "wide"), "narrow"),
            P(("groups", "wide"), "narrow"),
        ),
        check_vma=False,
    )
```

time: 66.8 us -> 28.4 us (0.43)
  blocking collectives: 48.9 us -> 0 us
  Pallas kernels: 0 us -> 23.5 us
  matrix products: 10.9 us -> 0 us
  other arithmetic: 1.13 us -> 0 us
  between operations: 1.5 us -> 0.64 us
    unnamed x1 -> x0, blocking collectives: 23.6 us -> none
    pallas_call x0 -> x1, Pallas kernels: none -> 23.5 us  [per_device(): pl.pallas_call(functools.partial(kernel, wide, narrow, kv_local, q_width,...]
    all_gather x1 -> x0, blocking collectives: 13.2 us -> none  [per_device(): lax.all_gather(heads, 'wide', axis=0, tiled=True)]
    psum x1 -> x0, blocking collectives: 12 us -> none  [per_device(): attn_out = lax.psum(request_out, 'narrow').astype(jnp.bfloat16)]
    dot_general x7 -> x0, matrix products: 10.9 us -> none  [the longest x1 4.72 us: per_device(): jnp.dot(rows, w_query, preferred_element_type=jnp.float32)]
    unnamed x22 -> x3, local copies, waits for them, and re-layouts: 0.68 us -> 3.98 us
    gather x3 -> x0, local copies, waits for them, and re-layouts: 2.77 us -> none  [the longest x1 1.51 us: per_device(): hidden[order[jnp.arange(slots_dev * lax.axis_size('wide'), dtype=jnp.int3...]
    select_n x2 -> x0, other arithmetic: 0.78 us -> none  [the longest x1 0.78 us: per_device(): jnp.zeros((requests,), jnp.int32).at[slot_of]]
where the time goes in v1:
time: 28.4 us; the launch traced here: 28.2 us
  Pallas kernels  23.5 us (83%)
  local copies, waits for them, and re-layouts  3.98 us (14%)
  between operations  0.64 us (2%)
    pallas_call x1, Pallas kernels, per_device(): pl.pallas_call(functools.partial(kernel, wide, narrow, kv_local, q_width,...  23.5 us
    unnamed x3, local copies, waits for them, and re-layouts  3.98 us

profile of v1, /device:TPU:0, one launch (start us, length us, event | category | flops | bytes accessed | tf_op | source)
XLA Modules:
  0.0 28.2 jit_solution(13363330428134468234)
XLA Ops:
  0.6 23.5 %decode_step.1 = (bf16[16,2048]{1,0:T(8,128)(2,1)}, bf16[4,256]{1,0:T(4,128)(2,1)}, bf16[4,256]{1,0:T(4,128)(2,1)}) custom-call(bf16[16,2048]{1,0:T(8,128)(2,1)} %hidden.1, bf16[2048,2048]{1,0:T(8,128)(2,1)} %w_query.1, bf16[2048,256]{1,0:T(8,128)(2,1)} %w_key.1, bf16[2048,256]{1,0:T(8,128)(2,1)} %w_value.1, bf16[2048,2048]{1,0:T(8,128)(2,1)} %w_out.1, ...), custom_call_target="tpu_custom_call" | custom-call | tf_op jit(solution)/shard_map/decode_step/pallas_call | solution.py:314
  24.2 1.5 %copy.16 = bf16[16,2048]{1,0:T(8,128)(2,1)} copy(bf16[16,2048]{1,0:T(8,128)(2,1)} %get-tuple-element.6) | data formatting | bytes 131072
  25.7 1.2 %copy.17 = bf16[4,256]{1,0:T(4,128)(2,1)} copy(bf16[4,256]{1,0:T(4,128)(2,1)} %get-tuple-element.7) | data formatting | bytes 4096
  26.9 1.3 %copy.18 = bf16[4,256]{1,0:T(4,128)(2,1)} copy(bf16[4,256]{1,0:T(4,128)(2,1)} %get-tuple-element.8) | data formatting | bytes 4096

commit v2 on v1

--- a/solution.py
+++ b/solution.py
@@ -24,19 +24,23 @@
     kv_local,
     q_width,
     o_width,
-    hidden,
+    hidden_in,
     w_query,
     w_key,
     w_value,
     w_out,
     key_cache,
     value_cache,
+    slot_row_in,
+    cycle_offset_in,
+    valid_length_in,
+    attn_out,
+    new_keys,
+    new_values,
+    hidden,
     slot_row,
     cycle_offset,
     valid_length,
-    attn_out,
-    new_keys,
-    new_values,
     wq,
     wk,
     wv,
@@ -44,15 +48,19 @@
     keys,
     values,
     part,
+    pair_got,
+    pair_sum,
     got,
     query_heads,
-    mixed_heads,
     heads_own,
     heads_got,
     heads_full,
     out_part,
     out_got,
     in_sem,
+    small_sem,
+    pair_send,
+    pair_recv,
     send_sem,
     recv_sem,
     head_send,
@@ -62,6 +70,9 @@
 ):
     me_wide = lax.axis_index("wide")
     me_narrow = lax.axis_index("narrow")
+    pairs = wide // 2
+    my_pair = me_wide // 2
+    side = me_wide - 2 * my_pair
     requests = hidden.shape[0]
     slots = keys.shape[0]
     head_dim = keys.shape[2]
@@ -93,10 +104,17 @@
         out_in.append(
             pltpu.make_async_copy(w_out.at[:, cols], wo.at[:, cols], in_sem.at[base + 2 + c])
         )
-    for copy in first:
+    small = [
+        pltpu.make_async_copy(hidden_in, hidden, small_sem.at[0]),
+        pltpu.make_async_copy(slot_row_in, slot_row, small_sem.at[1]),
+        pltpu.make_async_copy(cycle_offset_in, cycle_offset, small_sem.at[2]),
+        pltpu.make_async_copy(valid_length_in, valid_length, small_sem.at[3]),
+    ]
+    for copy in small + first:
         copy.start()
 
     barrier = pltpu.get_barrier_semaphore()
+    peers = wide + narrow - 2
     for d in range(1, wide):
         pl.semaphore_signal(
             barrier,
@@ -112,44 +130,75 @@
             device_id_type=MESH,
         )
 
+    small[0].wait()
+    small[1].wait()
     slot_id = lax.broadcasted_iota(jnp.int32, (requests, requests), 0)
     pick = jnp.where(slot_row[...] == slot_id, 1.0, 0.0)
     rows = jnp.dot(
         pick.astype(jnp.bfloat16), hidden[...], preferred_element_type=jnp.float32
     ).astype(jnp.bfloat16)
 
+    def to_neighbour(block, col, width):
+        return pltpu.make_async_remote_copy(
+            src_ref=part.at[1 - side, :, :, pl.ds(col, width)],
+            dst_ref=pair_got.at[:, :, pl.ds(col, width)],
+            send_sem=pair_send.at[block],
+            recv_sem=pair_recv.at[block],
+            device_id={"wide": 2 * my_pair + 1 - side},
+            device_id_type=MESH,
+        )
+
     def to_owner(block, d, col, width):
-        peer = lax.rem(me_wide + d, wide)
+        other = lax.rem(my_pair + d, pairs)
         return pltpu.make_async_remote_copy(
-            src_ref=part.at[peer, :, pl.ds(col, width)],
+            src_ref=pair_sum.at[other, :, pl.ds(col, width)],
             dst_ref=got.at[d, :, pl.ds(col, width)],
             send_sem=send_sem.at[block, d],
             recv_sem=recv_sem.at[block, d],
-            device_id={"wide": peer},
+            device_id={"wide": 2 * other + side},
             device_id_type=MESH,
         )
 
     blocks = [(query_cols, 2 * key_cols)] + [(c * q_width, q_width) for c in range(q_chunks)]
+
+    def keep(sums, col, width):
+        for w in range(wide):
+            part[w % 2, w // 2, :, col : col + width] = sums[w * slots : (w + 1) * slots]
+
+    def join(block):
+        col, width = blocks[block]
+        to_neighbour(block, col, width).wait_recv()
+        cols = slice(col, col + width)
+        pair_sum[:, :, cols] = part[side, :, :, cols] + pair_got[:, :, cols]
+        for d in range(1, pairs):
+            to_owner(block, d, col, width).start()
+
+    lag = 3
     for block, (col, width) in enumerate(blocks):
         if block == 0:
             first[0].wait()
-            sums = jnp.dot(rows, wk[...], preferred_element_type=jnp.float32)
-            for w in range(wide):
-                part[w, :, col : col + key_cols] = sums[w * slots : (w + 1) * slots]
+            keep(jnp.dot(rows, wk[...], preferred_element_type=jnp.float32), col, key_cols)
             first[1].wait()
-            sums = jnp.dot(rows, wv[...], preferred_element_type=jnp.float32)
-            for w in range(wide):
-                part[w, :, col + key_cols : col + width] = sums[w * slots : (w + 1) * slots]
-            pl.semaphore_wait(barrier, wide + narrow - 2)
+            keep(
+                jnp.dot(rows, wv[...], preferred_element_type=jnp.float32),
+                col + key_cols,
+                key_cols,
+            )
+            pl.semaphore_wait(barrier, peers)
         else:
             first[1 + block].wait()
-            sums = jnp.dot(rows, wq[:, col : col + width], preferred_element_type=jnp.float32)
-            for w in range(wide):
-                part[w, :, col : col + width] = sums[w * slots : (w + 1) * slots]
-        for d in range(1, wide):
-            to_owner(block, d, col, width).start()
+            keep(
+                jnp.dot(rows, wq[:, col : col + width], preferred_element_type=jnp.float32),
+                col,
+                width,
+            )
+        to_neighbour(block, col, width).start()
+        if block >= lag:
+            join(block - lag)
     for copy in cache_in + out_in:
         copy.start()
+    for block in range(max(len(blocks) - lag, 0), len(blocks)):
+        join(block)
 
     place = lax.broadcasted_iota(jnp.int32, (1, span), 1)
     position = place // kv_local
@@ -159,12 +208,12 @@
     scale = 1.0 / jnp.sqrt(jnp.float32(head_dim))
 
     def summed(col, width):
-        total = part[me_wide, :, col : col + width]
-        for d in range(1, wide):
+        total = pair_sum[my_pair, :, col : col + width]
+        for d in range(1, pairs):
             total = total + got[d, :, col : col + width]
         return total
 
-    for d in range(1, wide):
+    for d in range(1, pairs):
         to_owner(0, d, *blocks[0]).wait_recv()
     keys_new = summed(query_cols, key_cols).astype(jnp.bfloat16)
     values_new = summed(query_cols + key_cols, key_cols).astype(jnp.bfloat16)
@@ -174,12 +223,12 @@
     values_fresh = values_new.astype(jnp.float32)
     for block in range(1, len(blocks)):
         col, width = blocks[block]
-        for d in range(1, wide):
+        for d in range(1, pairs):
             to_owner(block, d, col, width).wait_recv()
         for h in range(col // head_dim, (col + width) // head_dim):
             query_heads[:, h, :] = summed(h * head_dim, head_dim)
 
-    for copy in cache_in:
+    for copy in cache_in + small[2:]:
         copy.wait()
 
     def by_head(fresh, s):
@@ -188,6 +237,16 @@
             other = fresh[s : s + 1, k * head_dim : (k + 1) * head_dim]
             result = jnp.where(row_kv == k, other, result)
         return result
+
+    def to_wide(s, d):
+        return pltpu.make_async_remote_copy(
+            src_ref=heads_own.at[s],
+            dst_ref=heads_got.at[d, s],
+            send_sem=head_send.at[s, d],
+            recv_sem=head_recv.at[s, d],
+            device_id={"wide": lax.rem(me_wide + d, wide)},
+            device_id_type=MESH,
+        )
 
     for s in range(slots):
         query = query_heads[s].astype(jnp.bfloat16)
@@ -214,34 +273,25 @@
             (spread * inverse).astype(jnp.bfloat16), values[s], preferred_element_type=jnp.float32
         )
         own_weight = (own * inverse).astype(jnp.bfloat16).astype(jnp.float32)
-        mixed_heads[s] = mixed + own_weight * by_head(values_fresh, s)
-
-    for h in range(heads_local):
-        heads_own[:, h * head_dim : (h + 1) * head_dim] = mixed_heads[:, h, :].astype(jnp.bfloat16)
-
-    def to_wide(d):
-        return pltpu.make_async_remote_copy(
-            src_ref=heads_own,
-            dst_ref=heads_got.at[d],
-            send_sem=head_send.at[d],
-            recv_sem=head_recv.at[d],
-            device_id={"wide": lax.rem(me_wide + d, wide)},
-            device_id_type=MESH,
-        )
-
-    for d in range(1, wide):
-        to_wide(d).start()
+        heads_own[s] = (mixed + own_weight * by_head(values_fresh, s)).astype(jnp.bfloat16)
+        for d in range(1, wide):
+            to_wide(s, d).start()
+
     heads_full[0:slots] = heads_own[...].astype(jnp.float32)
     for d in range(1, wide):
-        to_wide(d).wait_recv()
+        for s in range(slots):
+            to_wide(s, d).wait_recv()
         heads_full[d * slots : (d + 1) * slots] = heads_got[d].astype(jnp.float32)
     held_row = lax.broadcasted_iota(jnp.int32, (requests, requests), 0)
     back = held_row // slots
     held_slot = lax.rem(me_wide - back + wide, wide) * slots + (held_row - back * slots)
     give = jnp.where(slot_row[...] == held_slot, 1.0, 0.0).astype(jnp.bfloat16)
+    by_slot = jnp.concatenate(
+        [heads_full[:, h, :].astype(jnp.bfloat16) for h in range(heads_local)], axis=1
+    )
     heads = lax.dot_general(
         give,
-        heads_full[...].astype(jnp.bfloat16),
+        by_slot,
         (((0,), (0,)), ((), ())),
         preferred_element_type=jnp.float32,
     ).astype(jnp.bfloat16)
@@ -274,13 +324,21 @@
         attn_out[:, cols] = total.astype(jnp.bfloat16)
 
     for block, (col, width) in enumerate(blocks):
+        to_neighbour(block, col, width).wait_send()
+        for d in range(1, pairs):
+            to_owner(block, d, col, width).wait_send()
+    for s in range(slots):
         for d in range(1, wide):
-            to_owner(block, d, col, width).wait_send()
-    for d in range(1, wide):
-        to_wide(d).wait_send()
+            to_wide(s, d).wait_send()
     for c in range(o_chunks):
         for d in range(1, narrow):
             to_narrow(c, d).wait_send()
+
+
+def finish(attn, keys_new, values_new, attn_out, new_keys, new_values):
+    attn_out[...] = attn[...]
+    new_keys[...] = keys_new[...]
+    new_values[...] = values_new[...]
 
 
 def per_device(
@@ -309,43 +367,52 @@
     all_cols = query_cols + 2 * key_cols
     span = window * kv_local
     vmem = pl.BlockSpec(memory_space=pltpu.VMEM)
-    smem = pl.BlockSpec(memory_space=pltpu.SMEM)
-    anywhere = pl.BlockSpec(memory_space=pl.ANY)
-    return pl.pallas_call(
+    hbm = pl.BlockSpec(memory_space=pltpu.HBM)
+    heads_local = query_cols // head_dim
+    outs = (
+        jax.ShapeDtypeStruct((requests, out_cols), jnp.bfloat16),
+        jax.ShapeDtypeStruct((slots, key_cols), jnp.bfloat16),
+        jax.ShapeDtypeStruct((slots, key_cols), jnp.bfloat16),
+    )
+    results = pl.pallas_call(
         functools.partial(kernel, wide, narrow, kv_local, q_width, o_width),
-        out_shape=(
-            jax.ShapeDtypeStruct((requests, out_cols), jnp.bfloat16),
-            jax.ShapeDtypeStruct((slots, key_cols), jnp.bfloat16),
-            jax.ShapeDtypeStruct((slots, key_cols), jnp.bfloat16),
-        ),
-        in_specs=[vmem] + [anywhere] * 6 + [vmem, smem, smem],
+        out_shape=outs,
+        in_specs=[hbm] * 10,
         out_specs=(vmem, vmem, vmem),
         scratch_shapes=[
+            pltpu.VMEM(hidden.shape, jnp.bfloat16),
+            pltpu.VMEM((1, requests), jnp.int32),
+            pltpu.SMEM((slots,), jnp.int32),
+            pltpu.SMEM((slots,), jnp.int32),
             pltpu.VMEM(w_query.shape, jnp.bfloat16),
             pltpu.VMEM(w_key.shape, jnp.bfloat16),
             pltpu.VMEM(w_value.shape, jnp.bfloat16),
             pltpu.VMEM(w_out.shape, jnp.bfloat16),
             pltpu.VMEM((slots, span, head_dim), jnp.bfloat16),
             pltpu.VMEM((slots, span, head_dim), jnp.bfloat16),
-            pltpu.VMEM((wide, slots, all_cols), jnp.float32),
-            pltpu.VMEM((wide, slots, all_cols), jnp.float32),
-            pltpu.VMEM((slots, query_cols // head_dim, head_dim), jnp.float32),
-            pltpu.VMEM((slots, query_cols // head_dim, head_dim), jnp.float32),
-            pltpu.VMEM((slots, query_cols), jnp.bfloat16),
-            pltpu.VMEM((wide, slots, query_cols), jnp.bfloat16),
-            pltpu.VMEM((wide * slots, query_cols), jnp.float32),
+            pltpu.VMEM((2, wide // 2, slots, all_cols), jnp.float32),
+            pltpu.VMEM((wide // 2, slots, all_cols), jnp.float32),
+            pltpu.VMEM((wide // 2, slots, all_cols), jnp.float32),
+            pltpu.VMEM((wide // 2, slots, all_cols), jnp.float32),
+            pltpu.VMEM((slots, heads_local, head_dim), jnp.float32),
+            pltpu.VMEM((slots, heads_local, head_dim), jnp.bfloat16),
+            pltpu.VMEM((wide, slots, heads_local, head_dim), jnp.bfloat16),
+            pltpu.VMEM((wide * slots, heads_local, head_dim), jnp.float32),
             pltpu.VMEM((o_chunks, requests, o_width), jnp.bfloat16),
             pltpu.VMEM((o_chunks, narrow, requests, o_width), jnp.bfloat16),
             pltpu.SemaphoreType.DMA((4 + q_chunks + o_chunks,)),
-            pltpu.SemaphoreType.DMA((1 + q_chunks, wide)),
-            pltpu.SemaphoreType.DMA((1 + q_chunks, wide)),
-            pltpu.SemaphoreType.DMA((wide,)),
-            pltpu.SemaphoreType.DMA((wide,)),
+            pltpu.SemaphoreType.DMA((4,)),
+            pltpu.SemaphoreType.DMA((1 + q_chunks,)),
+            pltpu.SemaphoreType.DMA((1 + q_chunks,)),
+            pltpu.SemaphoreType.DMA((1 + q_chunks, wide // 2)),
+            pltpu.SemaphoreType.DMA((1 + q_chunks, wide // 2)),
+            pltpu.SemaphoreType.DMA((slots, wide)),
+            pltpu.SemaphoreType.DMA((slots, wide)),
             pltpu.SemaphoreType.DMA((o_chunks, narrow)),
             pltpu.SemaphoreType.DMA((o_chunks, narrow)),
         ],
         compiler_params=pltpu.CompilerParams(
-            collective_id=0, has_side_effects=True, vmem_limit_bytes=60 * 1024 * 1024
+            collective_id=0, has_side_effects=True, vmem_limit_bytes=63 * 1024 * 1024
         ),
         name="decode_step",
     )(
@@ -360,6 +427,13 @@
         cycle_offset,
         valid_length,
     )
+    return pl.pallas_call(
+        finish,
+        out_shape=outs,
+        in_specs=[vmem] * 3,
+        out_specs=(vmem,) * 3,
+        name="finish",
+    )(*results)
 
 
 def solution(mesh):

time: 28.4 us -> 29.1 us (1.025)
  Pallas kernels: 23.5 us -> 28.3 us
  local copies, waits for them, and re-layouts: 3.98 us -> 0 us
    unnamed x3 -> x0, local copies, waits for them, and re-layouts: 3.98 us -> none
    pallas_call x1, Pallas kernels: 23.5 us -> 26.8 us  [per_device(): pl.pallas_call(functools.partial(kernel, wide, narrow, kv_local, q_width,...]
    pallas_call x0 -> x1, Pallas kernels: none -> 1.48 us  [per_device(): pl.pallas_call(finish, out_shape=outs, in_specs=[vmem] * 3, out_specs=(vm...]
where the time goes in v2:
time: 29.1 us; the launch traced here: 28.9 us
  Pallas kernels  28.3 us (97%)
  between operations  0.64 us (2%)
    pallas_call x1, Pallas kernels, per_device(): pl.pallas_call(functools.partial(kernel, wide, narrow, kv_local, q_width,...  26.8 us
    pallas_call x1, Pallas kernels, per_device(): pl.pallas_call(finish, out_shape=outs, in_specs=[vmem] * 3, out_specs=(vm...  1.48 us

profile of v2, /device:TPU:0, one launch (start us, length us, event | category | flops | bytes accessed | tf_op | source)
XLA Modules:
  0.0 28.9 jit_solution(13230428499796481372)
XLA Ops:
  0.6 26.8 %decode_step.1 = (bf16[16,2048]{1,0:T(8,128)(2,1)}, bf16[4,256]{1,0:T(4,128)(2,1)}, bf16[4,256]{1,0:T(4,128)(2,1)}) custom-call(bf16[16,2048]{1,0:T(8,128)(2,1)} %hidden_in.1, bf16[2048,2048]{1,0:T(8,128)(2,1)} %w_query.1, bf16[2048,256]{1,0:T(8,128)(2,1)} %w_key.1, bf16[2048,256]{1,0:T(8,128)(2,1)} %w_value.1, bf16[2048,2048]{1,0:T(8,128)(2,1)} %w_out.1, ...), custom_call_target="tpu_custom_call" | custom-call | tf_op jit(solution)/shard_map/decode_step/pallas_call | solution.py:377
  27.4 1.5 %finish.1 = (bf16[16,2048]{1,0:T(8,128)(2,1)}, bf16[4,256]{1,0:T(4,128)(2,1)}, bf16[4,256]{1,0:T(4,128)(2,1)}) custom-call(bf16[16,2048]{1,0:T(8,128)(2,1)} %get-tuple-element.6.attn, bf16[4,256]{1,0:T(4,128)(2,1)} %get-tuple-element.7.keys_new, bf16[4,256]{1,0:T(4,128)(2,1)} %get-tuple-element.8.values_new), custom_call_target="tpu_custom_call" | custom-call | tf_op jit(solution)/shard_map/finish/pallas_call | solution.py:430

commit v3 on v2

--- a/solution.py
+++ b/solution.py
@@ -9,6 +9,8 @@
 
 masked_low = -1e30
 MESH = pl.DeviceIdType.MESH
+q_most = 1024
+o_most = 1024
 
 
 def width_of(columns, most):
@@ -48,10 +50,8 @@
     keys,
     values,
     part,
-    pair_got,
-    pair_sum,
     got,
-    query_heads,
+    queries,
     heads_own,
     heads_got,
     heads_full,
@@ -59,8 +59,6 @@
     out_got,
     in_sem,
     small_sem,
-    pair_send,
-    pair_recv,
     send_sem,
     recv_sem,
     head_send,
@@ -70,9 +68,6 @@
 ):
     me_wide = lax.axis_index("wide")
     me_narrow = lax.axis_index("narrow")
-    pairs = wide // 2
-    my_pair = me_wide // 2
-    side = me_wide - 2 * my_pair
     requests = hidden.shape[0]
     slots = keys.shape[0]
     head_dim = keys.shape[2]
@@ -138,67 +133,46 @@
         pick.astype(jnp.bfloat16), hidden[...], preferred_element_type=jnp.float32
     ).astype(jnp.bfloat16)
 
-    def to_neighbour(block, col, width):
+    def to_owner(block, d):
+        row, count = blocks[block]
+        peer = lax.rem(me_wide + d, wide)
         return pltpu.make_async_remote_copy(
-            src_ref=part.at[1 - side, :, :, pl.ds(col, width)],
-            dst_ref=pair_got.at[:, :, pl.ds(col, width)],
-            send_sem=pair_send.at[block],
-            recv_sem=pair_recv.at[block],
-            device_id={"wide": 2 * my_pair + 1 - side},
-            device_id_type=MESH,
-        )
-
-    def to_owner(block, d, col, width):
-        other = lax.rem(my_pair + d, pairs)
-        return pltpu.make_async_remote_copy(
-            src_ref=pair_sum.at[other, :, pl.ds(col, width)],
-            dst_ref=got.at[d, :, pl.ds(col, width)],
+            src_ref=part.at[peer, pl.ds(row, count)],
+            dst_ref=got.at[d, pl.ds(row, count)],
             send_sem=send_sem.at[block, d],
             recv_sem=recv_sem.at[block, d],
-            device_id={"wide": 2 * other + side},
+            device_id={"wide": peer},
             device_id_type=MESH,
         )
 
-    blocks = [(query_cols, 2 * key_cols)] + [(c * q_width, q_width) for c in range(q_chunks)]
-
-    def keep(sums, col, width):
-        for w in range(wide):
-            part[w % 2, w // 2, :, col : col + width] = sums[w * slots : (w + 1) * slots]
-
-    def join(block):
-        col, width = blocks[block]
-        to_neighbour(block, col, width).wait_recv()
-        cols = slice(col, col + width)
-        pair_sum[:, :, cols] = part[side, :, :, cols] + pair_got[:, :, cols]
-        for d in range(1, pairs):
-            to_owner(block, d, col, width).start()
-
-    lag = 3
-    for block, (col, width) in enumerate(blocks):
+    key_rows = key_cols // head_dim * slots
+    block_rows = q_width // head_dim * slots
+    first_query = 2 * key_rows
+    blocks = [(0, 2 * key_rows)] + [
+        (first_query + c * block_rows, block_rows) for c in range(q_chunks)
+    ]
+
+    def keep(sums, row):
+        for t in range(sums.shape[1] // head_dim):
+            tile = sums[:, t * head_dim : (t + 1) * head_dim]
+            for w in range(wide):
+                part[w, row + t * slots : row + (t + 1) * slots] = tile[w * slots : (w + 1) * slots]
+
+    for block, (row, count) in enumerate(blocks):
         if block == 0:
             first[0].wait()
-            keep(jnp.dot(rows, wk[...], preferred_element_type=jnp.float32), col, key_cols)
+            keep(jnp.dot(rows, wk[...], preferred_element_type=jnp.float32), 0)
             first[1].wait()
-            keep(
-                jnp.dot(rows, wv[...], preferred_element_type=jnp.float32),
-                col + key_cols,
-                key_cols,
-            )
+            keep(jnp.dot(rows, wv[...], preferred_element_type=jnp.float32), key_rows)
             pl.semaphore_wait(barrier, peers)
         else:
             first[1 + block].wait()
-            keep(
-                jnp.dot(rows, wq[:, col : col + width], preferred_element_type=jnp.float32),
-                col,
-                width,
-            )
-        to_neighbour(block, col, width).start()
-        if block >= lag:
-            join(block - lag)
+            cols = slice((block - 1) * q_width, block * q_width)
+            keep(jnp.dot(rows, wq[:, cols], preferred_element_type=jnp.float32), row)
+        for d in range(1, wide):
+            to_owner(block, d).start()
     for copy in cache_in + out_in:
         copy.start()
-    for block in range(max(len(blocks) - lag, 0), len(blocks)):
-        join(block)
 
     place = lax.broadcasted_iota(jnp.int32, (1, span), 1)
     position = place // kv_local
@@ -207,49 +181,47 @@
     same_head = row_kv == kv_of
     scale = 1.0 / jnp.sqrt(jnp.float32(head_dim))
 
-    def summed(col, width):
-        total = pair_sum[my_pair, :, col : col + width]
-        for d in range(1, pairs):
-            total = total + got[d, :, col : col + width]
+    def summed(block):
+        row, count = blocks[block]
+        total = part[me_wide, row : row + count]
+        for d in range(1, wide):
+            to_owner(block, d).wait_recv()
+            total = total + got[d, row : row + count]
         return total
 
-    for d in range(1, pairs):
-        to_owner(0, d, *blocks[0]).wait_recv()
-    keys_new = summed(query_cols, key_cols).astype(jnp.bfloat16)
-    values_new = summed(query_cols + key_cols, key_cols).astype(jnp.bfloat16)
-    new_keys[...] = keys_new
-    new_values[...] = values_new
-    keys_fresh = keys_new.astype(jnp.float32)
-    values_fresh = values_new.astype(jnp.float32)
+    fresh = summed(0).astype(jnp.bfloat16).astype(jnp.float32)
+    keys_fresh = fresh[:key_rows]
+    values_fresh = fresh[key_rows:]
+    for k in range(kv_local):
+        tile = slice(k * head_dim, (k + 1) * head_dim)
+        new_keys[:, tile] = keys_fresh[k * slots : (k + 1) * slots].astype(jnp.bfloat16)
+        new_values[:, tile] = values_fresh[k * slots : (k + 1) * slots].astype(jnp.bfloat16)
     for block in range(1, len(blocks)):
-        col, width = blocks[block]
-        for d in range(1, pairs):
-            to_owner(block, d, col, width).wait_recv()
-        for h in range(col // head_dim, (col + width) // head_dim):
-            query_heads[:, h, :] = summed(h * head_dim, head_dim)
+        row, count = blocks[block]
+        queries[row - first_query : row - first_query + count] = summed(block)
 
     for copy in cache_in + small[2:]:
         copy.wait()
 
     def by_head(fresh, s):
-        result = jnp.broadcast_to(fresh[s : s + 1, :head_dim], (heads_local, head_dim))
+        result = jnp.broadcast_to(fresh[s : s + 1], (heads_local, head_dim))
         for k in range(1, kv_local):
-            other = fresh[s : s + 1, k * head_dim : (k + 1) * head_dim]
+            other = fresh[k * slots + s : k * slots + s + 1]
             result = jnp.where(row_kv == k, other, result)
         return result
 
-    def to_wide(s, d):
+    def to_wide(d):
         return pltpu.make_async_remote_copy(
-            src_ref=heads_own.at[s],
-            dst_ref=heads_got.at[d, s],
-            send_sem=head_send.at[s, d],
-            recv_sem=head_recv.at[s, d],
+            src_ref=heads_own,
+            dst_ref=heads_got.at[d],
+            send_sem=head_send.at[d],
+            recv_sem=head_recv.at[d],
             device_id={"wide": lax.rem(me_wide + d, wide)},
             device_id_type=MESH,
         )
 
     for s in range(slots):
-        query = query_heads[s].astype(jnp.bfloat16)
+        query = queries[pl.ds(s, heads_local, stride=slots), :].astype(jnp.bfloat16)
         scores = (
             lax.dot_general(
                 query, keys[s], (((1,), (1,)), ((), ())), preferred_element_type=jnp.float32
@@ -274,13 +246,12 @@
         )
         own_weight = (own * inverse).astype(jnp.bfloat16).astype(jnp.float32)
         heads_own[s] = (mixed + own_weight * by_head(values_fresh, s)).astype(jnp.bfloat16)
-        for d in range(1, wide):
-            to_wide(s, d).start()
+    for d in range(1, wide):
+        to_wide(d).start()
 
     heads_full[0:slots] = heads_own[...].astype(jnp.float32)
     for d in range(1, wide):
-        for s in range(slots):
-            to_wide(s, d).wait_recv()
+        to_wide(d).wait_recv()
         heads_full[d * slots : (d + 1) * slots] = heads_got[d].astype(jnp.float32)
     held_row = lax.broadcasted_iota(jnp.int32, (requests, requests), 0)
     back = held_row // slots
@@ -323,13 +294,11 @@
             total = total + out_got[c, n].astype(jnp.float32)
         attn_out[:, cols] = total.astype(jnp.bfloat16)
 
-    for block, (col, width) in enumerate(blocks):
-        to_neighbour(block, col, width).wait_send()
-        for d in range(1, pairs):
-            to_owner(block, d, col, width).wait_send()
-    for s in range(slots):
+    for block in range(len(blocks)):
         for d in range(1, wide):
-            to_wide(s, d).wait_send()
+            to_owner(block, d).wait_send()
+    for d in range(1, wide):
+        to_wide(d).wait_send()
     for c in range(o_chunks):
         for d in range(1, narrow):
             to_narrow(c, d).wait_send()
@@ -360,11 +329,11 @@
     query_cols = w_query.shape[1]
     key_cols = w_key.shape[1]
     out_cols = w_out.shape[1]
-    q_width = width_of(query_cols, 512)
-    o_width = width_of(out_cols, 512)
+    q_width = width_of(query_cols, q_most)
+    o_width = width_of(out_cols, o_most)
     q_chunks = query_cols // q_width
     o_chunks = out_cols // o_width
-    all_cols = query_cols + 2 * key_cols
+    all_rows = (query_cols + 2 * key_cols) // head_dim * slots
     span = window * kv_local
     vmem = pl.BlockSpec(memory_space=pltpu.VMEM)
     hbm = pl.BlockSpec(memory_space=pltpu.HBM)
@@ -390,11 +359,9 @@
             pltpu.VMEM(w_out.shape, jnp.bfloat16),
             pltpu.VMEM((slots, span, head_dim), jnp.bfloat16),
             pltpu.VMEM((slots, span, head_dim), jnp.bfloat16),
-            pltpu.VMEM((2, wide // 2, slots, all_cols), jnp.float32),
-            pltpu.VMEM((wide // 2, slots, all_cols), jnp.float32),
-            pltpu.VMEM((wide // 2, slots, all_cols), jnp.float32),
-            pltpu.VMEM((wide // 2, slots, all_cols), jnp.float32),
-            pltpu.VMEM((slots, heads_local, head_dim), jnp.float32),
+            pltpu.VMEM((wide, all_rows, head_dim), jnp.float32),
+            pltpu.VMEM((wide, all_rows, head_dim), jnp.float32),
+            pltpu.VMEM((heads_local * slots, head_dim), jnp.float32),
             pltpu.VMEM((slots, heads_local, head_dim), jnp.bfloat16),
             pltpu.VMEM((wide, slots, heads_local, head_dim), jnp.bfloat16),
             pltpu.VMEM((wide * slots, heads_local, head_dim), jnp.float32),
@@ -402,12 +369,10 @@
             pltpu.VMEM((o_chunks, narrow, requests, o_width), jnp.bfloat16),
             pltpu.SemaphoreType.DMA((4 + q_chunks + o_chunks,)),
             pltpu.SemaphoreType.DMA((4,)),
-            pltpu.SemaphoreType.DMA((1 + q_chunks,)),
-            pltpu.SemaphoreType.DMA((1 + q_chunks,)),
-            pltpu.SemaphoreType.DMA((1 + q_chunks, wide // 2)),
-            pltpu.SemaphoreType.DMA((1 + q_chunks, wide // 2)),
-            pltpu.SemaphoreType.DMA((slots, wide)),
-            pltpu.SemaphoreType.DMA((slots, wide)),
+            pltpu.SemaphoreType.DMA((1 + q_chunks, wide)),
+            pltpu.SemaphoreType.DMA((1 + q_chunks, wide)),
+            pltpu.SemaphoreType.DMA((wide,)),
+            pltpu.SemaphoreType.DMA((wide,)),
             pltpu.SemaphoreType.DMA((o_chunks, narrow)),
             pltpu.SemaphoreType.DMA((o_chunks, narrow)),
         ],

time: 29.1 us -> 25 us (0.86)
  Pallas kernels: 28.3 us -> 24.2 us
    pallas_call x1, Pallas kernels: 26.8 us -> 22.7 us  [per_device(): pl.pallas_call(functools.partial(kernel, wide, narrow, kv_local, q_width,...]
where the time goes in v3:
time: 25 us; the launch traced here: 24.8 us
  Pallas kernels  24.2 us (97%)
  between operations  0.64 us (3%)
    pallas_call x1, Pallas kernels, per_device(): pl.pallas_call(functools.partial(kernel, wide, narrow, kv_local, q_width,...  22.7 us
    pallas_call x1, Pallas kernels, per_device(): pl.pallas_call(finish, out_shape=outs, in_specs=[vmem] * 3, out_specs=(vm...  1.48 us

profile of v3, /device:TPU:0, one launch (start us, length us, event | category | flops | bytes accessed | tf_op | source)
XLA Modules:
  0.0 24.8 jit_solution(11133026921623701793)
XLA Ops:
  0.6 22.7 %decode_step.1 = (bf16[16,2048]{1,0:T(8,128)(2,1)}, bf16[4,256]{1,0:T(4,128)(2,1)}, bf16[4,256]{1,0:T(4,128)(2,1)}) custom-call(bf16[16,2048]{1,0:T(8,128)(2,1)} %hidden_in.1, bf16[2048,2048]{1,0:T(8,128)(2,1)} %w_query.1, bf16[2048,256]{1,0:T(8,128)(2,1)} %w_key.1, bf16[2048,256]{1,0:T(8,128)(2,1)} %w_value.1, bf16[2048,2048]{1,0:T(8,128)(2,1)} %w_out.1, ...), custom_call_target="tpu_custom_call" | custom-call | tf_op jit(solution)/shard_map/decode_step/pallas_call | solution.py:346
  23.3 1.5 %finish.1 = (bf16[16,2048]{1,0:T(8,128)(2,1)}, bf16[4,256]{1,0:T(4,128)(2,1)}, bf16[4,256]{1,0:T(4,128)(2,1)}) custom-call(bf16[16,2048]{1,0:T(8,128)(2,1)} %get-tuple-element.6.attn, bf16[4,256]{1,0:T(4,128)(2,1)} %get-tuple-element.7.keys_new, bf16[4,256]{1,0:T(4,128)(2,1)} %get-tuple-element.8.values_new), custom_call_target="tpu_custom_call" | custom-call | tf_op jit(solution)/shard_map/finish/pallas_call | solution.py:395

commit v4 on v3

--- a/solution.py
+++ b/solution.py
@@ -9,7 +9,10 @@
 
 masked_low = -1e30
 MESH = pl.DeviceIdType.MESH
-q_most = 1024
+q_parts = (4, 4)
+finish_kib = 1024
+main_kib = 64512
+far = False
 o_most = 1024
 
 
@@ -20,11 +23,22 @@
     return width
 
 
+def blocks_of(columns, parts):
+    result, col, done = [], 0, 0
+    for share in parts:
+        done += share
+        end = columns // 128 * done // sum(parts) * 128
+        if end > col:
+            result.append((col, end - col))
+        col = end
+    return tuple(result)
+
+
 def kernel(
     wide,
     narrow,
     kv_local,
-    q_width,
+    q_blocks,
     o_width,
     hidden_in,
     w_query,
@@ -52,6 +66,7 @@
     part,
     got,
     queries,
+    allowed,
     heads_own,
     heads_got,
     heads_full,
@@ -78,15 +93,15 @@
     out_cols = wo.shape[1]
     heads_local = query_cols // head_dim
     group = heads_local // kv_local
-    q_chunks = query_cols // q_width
+    q_chunks = len(q_blocks)
     o_chunks = out_cols // o_width
 
     first = [
         pltpu.make_async_copy(w_key, wk, in_sem.at[0]),
         pltpu.make_async_copy(w_value, wv, in_sem.at[1]),
     ]
-    for c in range(q_chunks):
-        cols = pl.ds(c * q_width, q_width)
+    for c, (col, width) in enumerate(q_blocks):
+        cols = pl.ds(col, width)
         first.append(pltpu.make_async_copy(w_query.at[:, cols], wq.at[:, cols], in_sem.at[2 + c]))
     base = 2 + q_chunks
     cache_in = [
@@ -146,10 +161,10 @@
         )
 
     key_rows = key_cols // head_dim * slots
-    block_rows = q_width // head_dim * slots
     first_query = 2 * key_rows
     blocks = [(0, 2 * key_rows)] + [
-        (first_query + c * block_rows, block_rows) for c in range(q_chunks)
+        (first_query + col // head_dim * slots, width // head_dim * slots)
+        for col, width in q_blocks
     ]
 
     def keep(sums, row):
@@ -167,9 +182,9 @@
             pl.semaphore_wait(barrier, peers)
         else:
             first[1 + block].wait()
-            cols = slice((block - 1) * q_width, block * q_width)
-            keep(jnp.dot(rows, wq[:, cols], preferred_element_type=jnp.float32), row)
-        for d in range(1, wide):
+            col, width = q_blocks[block - 1]
+            keep(jnp.dot(rows, wq[:, col : col + width], preferred_element_type=jnp.float32), row)
+        for d in range(wide - 1, 0, -1) if far else range(1, wide):
             to_owner(block, d).start()
     for copy in cache_in + out_in:
         copy.start()
@@ -180,6 +195,14 @@
     row_kv = lax.broadcasted_iota(jnp.int32, (heads_local, 1), 0) // group
     same_head = row_kv == kv_of
     scale = 1.0 / jnp.sqrt(jnp.float32(head_dim))
+
+    for copy in small[2:]:
+        copy.wait()
+    for s in range(slots):
+        distance = cycle_offset[s] - position
+        distance = jnp.where(distance < 0, distance + window, distance)
+        usable = (distance > 0) & (distance < valid_length[s])
+        allowed[s] = jnp.where(usable & same_head, 1.0, 0.0)
 
     def summed(block):
         row, count = blocks[block]
@@ -200,7 +223,7 @@
         row, count = blocks[block]
         queries[row - first_query : row - first_query + count] = summed(block)
 
-    for copy in cache_in + small[2:]:
+    for copy in cache_in:
         copy.wait()
 
     def by_head(fresh, s):
@@ -220,32 +243,31 @@
             device_id_type=MESH,
         )
 
+    query, scores = [], []
     for s in range(slots):
-        query = queries[pl.ds(s, heads_local, stride=slots), :].astype(jnp.bfloat16)
-        scores = (
+        query.append(queries[pl.ds(s, heads_local, stride=slots), :].astype(jnp.bfloat16))
+        scores.append(
             lax.dot_general(
-                query, keys[s], (((1,), (1,)), ((), ())), preferred_element_type=jnp.float32
+                query[s], keys[s], (((1,), (1,)), ((), ())), preferred_element_type=jnp.float32
             )
             * scale
         )
+    weights, own_weight = [], []
+    for s in range(slots):
         own_score = (
-            jnp.sum(query.astype(jnp.float32) * by_head(keys_fresh, s), axis=1, keepdims=True)
+            jnp.sum(query[s].astype(jnp.float32) * by_head(keys_fresh, s), axis=1, keepdims=True)
             * scale
         )
-        offset = cycle_offset[s]
-        distance = offset - position
-        distance = jnp.where(distance < 0, distance + window, distance)
-        usable = (distance > 0) & (distance < valid_length[s])
-        masked = jnp.where(usable & same_head, scores, masked_low)
+        masked = jnp.where(allowed[s] > 0.0, scores[s], masked_low)
         top = jnp.maximum(jnp.max(masked, axis=1, keepdims=True), own_score)
         spread = jnp.exp(masked - top)
         own = jnp.exp(own_score - top)
         inverse = 1.0 / (jnp.sum(spread, axis=1, keepdims=True) + own)
-        mixed = jnp.dot(
-            (spread * inverse).astype(jnp.bfloat16), values[s], preferred_element_type=jnp.float32
-        )
-        own_weight = (own * inverse).astype(jnp.bfloat16).astype(jnp.float32)
-        heads_own[s] = (mixed + own_weight * by_head(values_fresh, s)).astype(jnp.bfloat16)
+        weights.append((spread * inverse).astype(jnp.bfloat16))
+        own_weight.append((own * inverse).astype(jnp.bfloat16).astype(jnp.float32))
+    for s in range(slots):
+        mixed = jnp.dot(weights[s], values[s], preferred_element_type=jnp.float32)
+        heads_own[s] = (mixed + own_weight[s] * by_head(values_fresh, s)).astype(jnp.bfloat16)
     for d in range(1, wide):
         to_wide(d).start()
 
@@ -329,9 +351,9 @@
     query_cols = w_query.shape[1]
     key_cols = w_key.shape[1]
     out_cols = w_out.shape[1]
-    q_width = width_of(query_cols, q_most)
+    q_blocks = blocks_of(query_cols, q_parts)
     o_width = width_of(out_cols, o_most)
-    q_chunks = query_cols // q_width
+    q_chunks = len(q_blocks)
     o_chunks = out_cols // o_width
     all_rows = (query_cols + 2 * key_cols) // head_dim * slots
     span = window * kv_local
@@ -344,8 +366,8 @@
         jax.ShapeDtypeStruct((slots, key_cols), jnp.bfloat16),
     )
     results = pl.pallas_call(
-        functools.partial(kernel, wide, narrow, kv_local, q_width, o_width),
-        out_shape=outs,
+        functools.partial(kernel, wide, narrow, kv_local, q_blocks, o_width),
+        out_shape=tuple(pltpu.VMEM(out.shape, out.dtype) for out in outs),
         in_specs=[hbm] * 10,
         out_specs=(vmem, vmem, vmem),
         scratch_shapes=[
@@ -362,6 +384,7 @@
             pltpu.VMEM((wide, all_rows, head_dim), jnp.float32),
             pltpu.VMEM((wide, all_rows, head_dim), jnp.float32),
             pltpu.VMEM((heads_local * slots, head_dim), jnp.float32),
+            pltpu.VMEM((slots, heads_local, span), jnp.float32),
             pltpu.VMEM((slots, heads_local, head_dim), jnp.bfloat16),
             pltpu.VMEM((wide, slots, heads_local, head_dim), jnp.bfloat16),
             pltpu.VMEM((wide * slots, heads_local, head_dim), jnp.float32),
@@ -377,7 +400,7 @@
             pltpu.SemaphoreType.DMA((o_chunks, narrow)),
         ],
         compiler_params=pltpu.CompilerParams(
-            collective_id=0, has_side_effects=True, vmem_limit_bytes=63 * 1024 * 1024
+            collective_id=0, has_side_effects=True, vmem_limit_bytes=main_kib * 1024
         ),
         name="decode_step",
     )(
@@ -397,6 +420,7 @@
         out_shape=outs,
         in_specs=[vmem] * 3,
         out_specs=(vmem,) * 3,
+        compiler_params=pltpu.CompilerParams(vmem_limit_bytes=finish_kib * 1024),
         name="finish",
     )(*results)
 

time: 25 us -> 22.5 us (0.900)
  Pallas kernels: 24.2 us -> 21.7 us
    pallas_call x1, Pallas kernels: 22.7 us -> 21 us  [per_device(): pl.pallas_call(functools.partial(kernel, wide, narrow, kv_local, q_blocks...]
    pallas_call x1, Pallas kernels: 1.48 us -> 0.64 us  [per_device(): pl.pallas_call(finish, out_shape=outs, in_specs=[vmem] * 3, out_specs=(vm...]
where the time goes in v4:
time: 22.5 us; the launch traced here: 22.3 us
  Pallas kernels  21.7 us (96%)
  between operations  0.64 us (3%)
    pallas_call x1, Pallas kernels, per_device(): pl.pallas_call(functools.partial(kernel, wide, narrow, kv_local, q_blocks...  21 us
    pallas_call x1, Pallas kernels, per_device(): pl.pallas_call(finish, out_shape=outs, in_specs=[vmem] * 3, out_specs=(vm...  0.64 us

profile of v4, /device:TPU:0, one launch (start us, length us, event | category | flops | bytes accessed | tf_op | source)
XLA Modules:
  0.0 22.3 jit_solution(18070717705459707149)
XLA Ops:
  0.6 21.0 %decode_step.1 = (bf16[16,2048]{1,0:T(8,128)(2,1)S(1)}, bf16[4,256]{1,0:T(4,128)(2,1)S(1)}, bf16[4,256]{1,0:T(4,128)(2,1)S(1)}) custom-call(bf16[16,2048]{1,0:T(8,128)(2,1)} %hidden_in.1, bf16[2048,2048]{1,0:T(8,128)(2,1)} %w_query.1, bf16[2048,256]{1,0:T(8,128)(2,1)} %w_key.1, bf16[2048,256]{1,0:T(8,128)(2,1)} %w_value.1, bf16[2048,2048]{1,0:T(8,128)(2,1)} %w_out.1, ...), custom_call_target="tpu_custom_call" | custom-call | tf_op jit(solution)/shard_map/decode_step/pallas_call | solution.py:368
  21.7 0.6 %finish.1 = (bf16[16,2048]{1,0:T(8,128)(2,1)}, bf16[4,256]{1,0:T(4,128)(2,1)}, bf16[4,256]{1,0:T(4,128)(2,1)}) custom-call(bf16[16,2048]{1,0:T(8,128)(2,1)S(1)} %get-tuple-element.6.attn, bf16[4,256]{1,0:T(4,128)(2,1)S(1)} %get-tuple-element.7.keys_new, bf16[4,256]{1,0:T(4,128)(2,1)S(1)} %get-tuple-element.8.values_new), custom_call_target="tpu_custom_call" | custom-call | tf_op jit(solution)/shard_map/finish/pallas_call | solution.py:418
